TPU v7x, 256 devices: a whole 4x4x8 slice. The times are simulated.
256 devices in a mesh: src: 2 (over z_hi), gx: 8 (over z_lo, core), gy: 16 (over y, x).
Axes of the slice: x: 4, y: 4, z: 8 (z_hi: 2, z_lo: 4; z = z_hi * 4 + z_lo), core: 2. Of those that a mesh axis runs over, the one named last changes fastest.
Arguments:
- forward_state: float32 [4, 6, 128, 65536], P('src', None, 'gx', 'gy'), may hold values from -6 to 6
- adjoint_state: float32 [4, 6, 128, 65536], P('src', None, 'gx', 'gy'), may hold values from -6 to 6
- permittivity: float32 [128, 65536], P('gx', 'gy'), may hold values from 1 to 3
- waveform: float32 [4, 4], P('src'), may hold values from -8 to 8
- source_cell: int32 [4, 3], P('src'), may hold values from 0 to 1023, as said below
- block_owner: int32 [32, 256], P('gx', 'gy'), may hold values from -1 to 15, as said below
- block_slot: int32 [32, 256], P('gx', 'gy'), may hold values from -1 to 3, as said below
- owner_rows: int32 [128, 64], P(('gx', 'gy')), may hold values from 0 to 63, as said below
Outputs:
- design_gradient: float32 [8192, 1024], P(('gx', 'gy'), 'src')
Inputs may be any that keep to these rules, and one draw needn't show every extreme that they name: `block_owner`: -1 marks a block outside the design region; otherwise the owner lies in the block's own gx row. The design blocks of one device that go to one owner number at most 4, and some device sends exactly 4 to some owner. `block_slot`: -1 exactly where block_owner is -1; the blocks that one device sends to one owner have distinct slots. `owner_rows`: each row is a permutation of 0 to 63. `source_cell`: each row is a cell (x, y, z) of the grid.
All inputs are finite; a program needn't handle non-finite values.
Results may differ from a plain program's by a relative error of at most 0.0003.
Values sent between devices are 32-bit elements; how exact they have to be, the bound alone decides.
No kernel may reach another device: no remote copies, remote signals or barrier semaphores. Data moves between devices by JAX's collectives and lax.ppermute only.
A program may use at most 128 MiB of HBM per device.

v0:
```python
import jax
import jax.numpy as jnp
from jax import lax
from jax.sharding import PartitionSpec as P

NZ = 64
STEPS = 4
BX = 4
BY = 4
courant = 0.55


def passed_along(shard, axis, by):
    count = lax.axis_size(axis)
    pairs = [(i, i + by) for i in range(count) if 0 <= i + by < count]
    return lax.ppermute(shard, axis, pairs)


def upper_z(values, z_cells):
    zindex = lax.broadcasted_iota(jnp.int32, values.shape, values.ndim - 1) % z_cells
    shifted = jnp.concatenate([values[..., 1:], jnp.zeros_like(values[..., :1])], axis=-1)
    return jnp.where(zindex == z_cells - 1, jnp.zeros_like(shifted), shifted)


def lower_z(values, z_cells):
    zindex = lax.broadcasted_iota(jnp.int32, values.shape, values.ndim - 1) % z_cells
    shifted = jnp.concatenate([jnp.zeros_like(values[..., :1]), values[..., :-1]], axis=-1)
    return jnp.where(zindex == 0, jnp.zeros_like(shifted), shifted)


def upper_x(values, ghosts):
    return jnp.concatenate([values[..., 1:, :], ghosts], axis=-2)


def lower_x(values, ghosts):
    return jnp.concatenate([ghosts, values[..., :-1, :]], axis=-2)


def upper_y(values, ghosts, z_cells):
    return jnp.concatenate([values[..., z_cells:], ghosts], axis=-1)


def lower_y(values, ghosts, z_cells):
    return jnp.concatenate([ghosts, values[..., :-z_cells]], axis=-1)


def magnetic_update(electric, magnetic, ghost_x, ghost_y, z_cells):
    new_hx = magnetic[0] - courant * (
        upper_y(electric[2], ghost_y[1], z_cells)
        - electric[2]
        - (upper_z(electric[1], z_cells) - electric[1])
    )
    new_hy = magnetic[1] - courant * (
        upper_z(electric[0], z_cells)
        - electric[0]
        - (upper_x(electric[2], ghost_x[1]) - electric[2])
    )
    new_hz = magnetic[2] - courant * (
        upper_x(electric[1], ghost_x[0])
        - electric[1]
        - (upper_y(electric[0], ghost_y[0], z_cells) - electric[0])
    )
    return (new_hx, new_hy, new_hz)


def electric_update(electric, magnetic, ghost_x, ghost_y, factor, z_cells):
    new_ex = electric[0] + factor * (
        magnetic[2]
        - lower_y(magnetic[2], ghost_y[1], z_cells)
        - (magnetic[1] - lower_z(magnetic[1], z_cells))
    )
    new_ey = electric[1] + factor * (
        magnetic[0]
        - lower_z(magnetic[0], z_cells)
        - (magnetic[2] - lower_x(magnetic[2], ghost_x[1]))
    )
    new_ez = electric[2] + factor * (
        magnetic[1]
        - lower_x(magnetic[1], ghost_x[0])
        - (magnetic[0] - lower_y(magnetic[0], ghost_y[0], z_cells))
    )
    return (new_ex, new_ey, new_ez)


def upper_ghosts(electric, z_cells):
    planes = jnp.stack([electric[1][:, :1, :], electric[2][:, :1, :]], axis=1)
    planes = passed_along(planes, "gx", -1)
    strips = jnp.stack([electric[0][..., :z_cells], electric[2][..., :z_cells]], axis=1)
    flat_strips = passed_along(strips.reshape(strips.shape[0], 2, -1), "gy", -1)
    strips = flat_strips.reshape(strips.shape)
    return ((planes[:, 0], planes[:, 1]), (strips[:, 0], strips[:, 1]))


def lower_ghosts(magnetic, z_cells):
    planes = jnp.stack([magnetic[1][:, -1:, :], magnetic[2][:, -1:, :]], axis=1)
    planes = passed_along(planes, "gx", 1)
    strips = jnp.stack([magnetic[0][..., -z_cells:], magnetic[2][..., -z_cells:]], axis=1)
    flat_strips = passed_along(strips.reshape(strips.shape[0], 2, -1), "gy", 1)
    strips = flat_strips.reshape(strips.shape)
    return ((planes[:, 0], planes[:, 1]), (strips[:, 0], strips[:, 1]))


def advance(electric, magnetic, factor, z_cells):
    ghost_x, ghost_y = upper_ghosts(electric, z_cells)
    magnetic = magnetic_update(electric, magnetic, ghost_x, ghost_y, z_cells)
    ghost_x, ghost_y = lower_ghosts(magnetic, z_cells)
    electric = electric_update(electric, magnetic, ghost_x, ghost_y, factor, z_cells)
    return (electric, magnetic)


def per_device(
    forward_state,
    adjoint_state,
    permittivity,
    waveform,
    source_cell,
    block_owner,
    block_slot,
    owner_rows,
):
    cells_x = permittivity.shape[0]
    cells_yz = permittivity.shape[1]
    cells_y = cells_yz // NZ
    factor = courant / permittivity
    x_index = lax.broadcasted_iota(jnp.int32, (cells_x, cells_yz), 0)
    yz_index = lax.broadcasted_iota(jnp.int32, (cells_x, cells_yz), 1)
    local_x = source_cell[:, 0] - lax.axis_index("gx") * cells_x
    local_yz = (source_cell[:, 1] - lax.axis_index("gy") * cells_y) * NZ + source_cell[:, 2]
    beacon = (
        (x_index[None] == local_x[:, None, None]) & (yz_index[None] == local_yz[:, None, None])
    ).astype(jnp.float32)
    density = jnp.zeros((cells_x, cells_yz), jnp.float32)
    electric = (forward_state[:, 0], forward_state[:, 1], forward_state[:, 2])
    magnetic = (forward_state[:, 3], forward_state[:, 4], forward_state[:, 5])
    increments = []
    for step_index in range(STEPS):
        updated, magnetic = advance(electric, magnetic, factor, NZ)
        updated = (
            updated[0],
            updated[1],
            updated[2] + waveform[:, step_index][:, None, None] * beacon,
        )
        increments.append(
            (updated[0] - electric[0], updated[1] - electric[1], updated[2] - electric[2])
        )
        electric = updated
    electric = (adjoint_state[:, 0], adjoint_state[:, 1], adjoint_state[:, 2])
    magnetic = (adjoint_state[:, 3], adjoint_state[:, 4], adjoint_state[:, 5])
    for step_index in range(STEPS):
        electric, magnetic = advance(electric, magnetic, factor, NZ)
        paired = increments[STEPS - 1 - step_index]
        intersection = electric[0] * paired[0] + electric[1] * paired[1] + electric[2] * paired[2]
        density = density + jnp.sum(intersection, axis=0)
    gradient = -density / permittivity
    blocks = (
        gradient.reshape(cells_x // BX, BX, cells_y // BY, BY, NZ)
        .transpose(0, 2, 1, 3, 4)
        .reshape(-1, BX * BY * NZ)
    )
    owners = block_owner.reshape(-1)
    slots = block_slot.reshape(-1)
    peers = lax.axis_size("gy")
    capacity = max(2, (blocks.shape[0] + peers - 1) // peers)
    rows_owned = peers * capacity
    destination = jnp.where(owners >= 0, owners * capacity + slots, rows_owned)
    outgoing = (
        jnp.zeros((rows_owned, blocks.shape[1]), jnp.float32)
        .at[destination]
        .set(blocks, mode="drop")
    )
    sectioned = outgoing.reshape(peers, capacity, 1, -1)
    arrived = lax.all_to_all(
        lax.all_to_all(sectioned, "src", split_axis=3, concat_axis=2, tiled=True),
        "gy",
        split_axis=0,
        concat_axis=0,
        tiled=True,
    )
    arrived = jnp.sum(arrived, axis=2)
    placed = jnp.zeros((rows_owned, arrived.shape[-1]), jnp.float32)
    return placed.at[owner_rows[0]].set(arrived.reshape(rows_owned, -1))


def solution(mesh):
    in_specs = (
        P("src", None, "gx", "gy"),
        P("src", None, "gx", "gy"),
        P("gx", "gy"),
        P("src", None),
        P("src", None),
        P("gx", "gy"),
        P("gx", "gy"),
        P(("gx", "gy"), None),
    )
    out_specs = P(("gx", "gy"), "src")
    return jax.shard_map(
        per_device, mesh=mesh, in_specs=in_specs, out_specs=out_specs, check_vma=False
    )
```

profile of v0, /device:TPU:32, one launch (start us, length us, event | category | flops | bytes accessed | tf_op | source)
XLA Modules:
  0.0 353.1 jit_solution(7784408515119125524)
XLA Ops:
  7.9 3.8 %collective-permute-start = (f32[2,2,1,4096]{3,1,2,0:T(2,128)}, f32[2,2,1,4096]{3,1,2,0:T(2,128)}, u32[]{:S(2)}, u32[]{:S(2)}) collective-permute-start(f32[2,2,1,4096]{3,1,2,0:T(2,128)} %pad_maximum_fusion), channel_id=1, source_target_pairs={{16,0},{32,16},{48,32},{64,48},{80,64},{96,80},{112,96},{17,1},{33... | collective-permute-start | bytes 196616 | tf_op jit(solution)/shard_map/ppermute | solution.py:16
  36.8 5.5 %collective-permute-start.5 = (f32[2,2,1024]{2,0,1:T(2,128)}, f32[2,2,1024]{2,0,1:T(2,128)}, u32[]{:S(2)}, u32[]{:S(2)}) collective-permute-start(f32[2,2,1024]{2,0,1:T(2,128)} %pad_maximum_fusion.19), channel_id=1, source_target_pairs={{0,1},{1,2},{2,3},{3,4},{4,5},{5,6},{6,7},{7,8},{8,9},{9,10},{10,1... | collective-permute-start | bytes 49160 | tf_op jit(solution)/shard_map/ppermute | solution.py:16
  45.0 2.7 fusion.102
  51.8 3.3 collective-permute-start.2
  69.6 2.4 collective-permute-start.7
  74.0 2.5 fusion.118
  77.7 4.5 %collective-permute-start.9 = (f32[2,2,1024]{2,0,1:T(2,128)S(1)}, f32[2,2,1024]{2,0,1:T(2,128)S(1)}, u32[]{:S(2)}, u32[]{:S(2)}) collective-permute-start(f32[2,2,1024]{2,0,1:T(2,128)S(1)} %pad_maximum_fusion.21), channel_id=1, source_target_pairs={{0,1},{1,2},{2,3},{3,4},{4,5},{5,6},{6,7},{7,8},{8,9},{9,10},{10,1... | collective-permute-start | bytes 49160 | tf_op jit(solution)/shard_map/ppermute | solution.py:16
  82.4 3.5 collective-permute-start.10
  110.1 3.6 %fusion.126 = (f32[2,16,4096]{2,1,0:T(8,128)S(1)}, f32[2,16,4096]{2,1,0:T(8,128)}, f32[2,16,4096]{2,1,0:T(8,128)S(1)}) fusion(f32[2,16,4096]{2,1,0:T(8,128)} %copy-done.9, f32[2,16,4096]{2,1,0:T(8,128)S(1)} %get-tuple-element.36, f32[2,16,4096]{2,1,0:T(8,128)S(1)} %fusion.184, f32[2,16,64]{2,1,0:T(8,128)S(1)} %get-tuple-element.110, ...), kind=kLoop, calls=%fused_computation.132 | loop fusion | flops 3014656 | bytes 7900928 | tf_op jit(solution)/shard_map/sub | solution.py:48
  114.9 5.1 %collective-permute-start.13 = (f32[2,2,1024]{2,0,1:T(2,128)S(1)}, f32[2,2,1024]{2,0,1:T(2,128)S(1)}, u32[]{:S(2)}, u32[]{:S(2)}) collective-permute-start(f32[2,2,1024]{2,0,1:T(2,128)S(1)} %pad_maximum_fusion.23), channel_id=1, source_target_pairs={{0,1},{1,2},{2,3},{3,4},{4,5},{5,6},{6,7},{7,8},{8,9},{9,10},{10,1... | collective-permute-start | bytes 49160 | tf_op jit(solution)/shard_map/ppermute | solution.py:16
  121.1 3.7 %collective-permute-start.14 = (f32[2,2,1,4096]{3,1,2,0:T(2,128)S(1)}, f32[2,2,1,4096]{3,1,2,0:T(2,128)S(1)}, u32[]{:S(2)}, u32[]{:S(2)}) collective-permute-start(f32[2,2,1,4096]{3,1,2,0:T(2,128)S(1)} %pad_maximum_fusion.6), channel_id=1, source_target_pairs={{0,16},{16,32},{32,48},{48,64},{64,80},{80,96},{96,112},{1,17},{17... | collective-permute-start | bytes 196616 | tf_op jit(solution)/shard_map/ppermute | solution.py:16
  150.3 3.0 fusion.134
  158.9 5.4 %collective-permute-start.17 = (f32[2,2,1024]{2,0,1:T(2,128)S(1)}, f32[2,2,1024]{2,0,1:T(2,128)}, u32[]{:S(2)}, u32[]{:S(2)}) collective-permute-start(f32[2,2,1024]{2,0,1:T(2,128)S(1)} %pad_maximum_fusion.25), channel_id=1, source_target_pairs={{0,1},{1,2},{2,3},{3,4},{4,5},{5,6},{6,7},{7,8},{8,9},{9,10},{10,1... | collective-permute-start | bytes 49160 | tf_op jit(solution)/shard_map/ppermute | solution.py:16
  165.8 3.7 %collective-permute-start.19 = (f32[2,2,1,4096]{3,1,2,0:T(2,128)}, f32[2,2,1,4096]{3,1,2,0:T(2,128)}, u32[]{:S(2)}, u32[]{:S(2)}) collective-permute-start(f32[2,2,1,4096]{3,1,2,0:T(2,128)} %pad_maximum_fusion.9), channel_id=1, source_target_pairs={{0,16},{16,32},{32,48},{48,64},{64,80},{80,96},{96,112},{1,17},{17... | collective-permute-start | bytes 196616 | tf_op jit(solution)/shard_map/ppermute | solution.py:16
  172.7 6.4 %fusion.166 = (f32[16,4096]{1,0:T(8,128)}, f32[2,16,4096]{2,1,0:T(8,128)S(1)}, f32[2,16,4096]{2,1,0:T(8,128)S(1)}, f32[2,16,4096]{2,1,0:T(8,128)S(1)}) fusion(f32[2,16,4096]{2,1,0:T(8,128)} %get-tuple-element.35, f32[2,16,4096]{2,1,0:T(8,128)} %copy-done.48, f32[2,16,4096]{2,1,0:T(8,128)S(1)} %get-tuple-element.34, f32[2,16,4096]{2,1,0:T(8,128)} %copy-done.50, ...), kind=kLoop, calls=%fused_computation.172 | loop fusion | flops 7536640 | bytes 14716440 | tf_op jit(solution)/shard_map/reduce_sum | solution.py:153
  195.6 4.1 %fusion.142 = (f32[2,16,4096]{2,1,0:T(8,128)S(1)}, f32[2,16,4096]{2,1,0:T(8,128)}, f32[2,16,4096]{2,1,0:T(8,128)S(1)}) fusion(f32[2,16,4096]{2,1,0:T(8,128)} %copy-done.37, f32[2,16,4096]{2,1,0:T(8,128)} %copy-done.33, f32[2,16,4096]{2,1,0:T(8,128)} %copy-done.20, f32[2,16,64]{2,1,0:T(8,128)S(1)} %get-tuple-element.98, f32[2,16,4032]{2,1,0:T(8,128)} %slice.1120, ...), kind=kLoop, calls=%fused_computation.148 | loop fusion | flops 3014656 | bytes 7900928 | tf_op jit(solution)/shard_map/sub | solution.py:48
  200.9 6.7 %collective-permute-start.22 = (f32[2,2,1024]{2,0,1:T(2,128)S(1)}, f32[2,2,1024]{2,0,1:T(2,128)}, u32[]{:S(2)}, u32[]{:S(2)}) collective-permute-start(f32[2,2,1024]{2,0,1:T(2,128)S(1)} %pad_maximum_fusion.27), channel_id=1, source_target_pairs={{0,1},{1,2},{2,3},{3,4},{4,5},{5,6},{6,7},{7,8},{8,9},{9,10},{10,1... | collective-permute-start | bytes 49160 | tf_op jit(solution)/shard_map/ppermute | solution.py:16
  209.3 3.6 %collective-permute-start.23 = (f32[2,2,1,4096]{3,1,2,0:T(2,128)}, f32[2,2,1,4096]{3,1,2,0:T(2,128)S(1)}, u32[]{:S(2)}, u32[]{:S(2)}) collective-permute-start(f32[2,2,1,4096]{3,1,2,0:T(2,128)} %pad_maximum_fusion.11), channel_id=1, source_target_pairs={{0,16},{16,32},{32,48},{48,64},{64,80},{80,96},{96,112},{1,17},{17... | collective-permute-start | bytes 196616 | tf_op jit(solution)/shard_map/ppermute | solution.py:16
  234.8 4.1 %fusion.150 = (f32[2,16,4096]{2,1,0:T(8,128)S(1)}, f32[2,16,4096]{2,1,0:T(8,128)}, f32[2,16,4096]{2,1,0:T(8,128)S(1)}) fusion(f32[2,16,4096]{2,1,0:T(8,128)} %copy-done.7, f32[2,16,4096]{2,1,0:T(8,128)} %copy-done.36, f32[2,16,4096]{2,1,0:T(8,128)} %copy-done.18, f32[2,16,64]{2,1,0:T(8,128)S(1)} %get-tuple-element.94, f32[2,16,4032]{2,1,0:T(8,128)} %slice.1148, ...), kind=kLoop, calls=%fused_computation.156 | loop fusion | flops 3014656 | bytes 7900928 | tf_op jit(solution)/shard_map/sub | solution.py:48
  240.1 6.7 %collective-permute-start.26 = (f32[2,2,1024]{2,0,1:T(2,128)S(1)}, f32[2,2,1024]{2,0,1:T(2,128)}, u32[]{:S(2)}, u32[]{:S(2)}) collective-permute-start(f32[2,2,1024]{2,0,1:T(2,128)S(1)} %pad_maximum_fusion.29), channel_id=1, source_target_pairs={{0,1},{1,2},{2,3},{3,4},{4,5},{5,6},{6,7},{7,8},{8,9},{9,10},{10,1... | collective-permute-start | bytes 49160 | tf_op jit(solution)/shard_map/ppermute | solution.py:16
  248.5 3.6 %collective-permute-start.27 = (f32[2,2,1,4096]{3,1,2,0:T(2,128)}, f32[2,2,1,4096]{3,1,2,0:T(2,128)S(1)}, u32[]{:S(2)}, u32[]{:S(2)}) collective-permute-start(f32[2,2,1,4096]{3,1,2,0:T(2,128)} %pad_maximum_fusion.13), channel_id=1, source_target_pairs={{0,16},{16,32},{32,48},{48,64},{64,80},{80,96},{96,112},{1,17},{17... | collective-permute-start | bytes 196616 | tf_op jit(solution)/shard_map/ppermute | solution.py:16
  254.3 5.4 %add_reduce_fusion.1 = (f32[16,4096]{1,0:T(8,128)}, f32[16,4096]{1,0:T(8,128)}, f32[2,16,4096]{2,1,0:T(8,128)S(1)}, f32[2,16,4096]{2,1,0:T(8,128)S(1)}, f32[2,16,4096]{2,1,0:T(8,128)S(1)}) fusion(f32[2,16,4096]{2,1,0:T(8,128)} %copy-done.18, f32[2,16,4096]{2,1,0:T(8,128)S(1)} %fusion.191, f32[2,16,4096]{2,1,0:T(8,128)S(1)} %fusion.184, ...), kind=kLoop, calls=%fused_computation.295 | loop fusion | flops 5242880 | bytes 13405952 | tf_op jit(solution)/shard_map/reduce_sum | solution.py:153
  276.2 2.8 fusion.158
  280.4 6.1 %collective-permute-start.30 = (f32[2,2,1024]{2,0,1:T(2,128)S(1)}, f32[2,2,1024]{2,0,1:T(2,128)S(1)}, u32[]{:S(2)}, u32[]{:S(2)}) collective-permute-start(f32[2,2,1024]{2,0,1:T(2,128)S(1)} %pad_maximum_fusion.31), channel_id=1, source_target_pairs={{0,1},{1,2},{2,3},{3,4},{4,5},{5,6},{6,7},{7,8},{8,9},{9,10},{10,1... | collective-permute-start | bytes 49160 | tf_op jit(solution)/shard_map/ppermute | solution.py:16
  286.6 4.0 %collective-permute-start.31 = (f32[2,2,1,4096]{3,1,2,0:T(2,128)S(1)}, f32[2,2,1,4096]{3,1,2,0:T(2,128)S(1)}, u32[]{:S(2)}, u32[]{:S(2)}) collective-permute-start(f32[2,2,1,4096]{3,1,2,0:T(2,128)S(1)} %pad_maximum_fusion.15), channel_id=1, source_target_pairs={{0,16},{16,32},{32,48},{48,64},{64,80},{80,96},{96,112},{1,17},{17... | collective-permute-start | bytes 196616 | tf_op jit(solution)/shard_map/ppermute | solution.py:16
  292.2 4.2 %fusion.93 = f32[16,4096]{1,0:T(8,128)S(1)} fusion(f32[2,16,4096]{2,1,0:T(8,128)} %copy-done.39, f32[2,16,4096]{2,1,0:T(8,128)} %copy-done.49, f32[2,16,4096]{2,1,0:T(8,128)} %copy-done.31, f32[2,16,4096]{2,1,0:T(8,128)} %copy-done.51, f32[2,16,4096]{2,1,0:T(8,128)} %copy-done.47, f32[2,16,4032]{2,1,0:T(8,128)} %bitcast.413, ...), kind=kLoop, calls=%fused_computation.99 | loop fusion | flops 4128768 | bytes 9998080 | tf_op jit(solution)/shard_map/reduce_sum | solution.py:153
  300.3 2.9 reshape.295
  303.2 17.4 %all_to_all.17 = f32[2,1,32768]{2,1,0:T(1,128)S(1)} all-to-all(f32[2,1,32768]{2,1,0:T(1,128)S(1)} %reshape.295), channel_id=1, replica_groups=mesh['src'=2,'gx'=8,'gy'=16] {'src'}, dimensions={0} | all-to-all | bytes 524288 | tf_op jit(solution)/shard_map/all_to_all | solution.py:173
  322.6 2.8 reshape.296
  325.4 2.5 copy.86
  327.9 15.0 %all-to-all-start.1 = ((f32[16,4,2,512]{3,1,2,0:T(4,128)}), f32[16,4,2,512]{3,1,2,0:T(4,128)S(1)}, u32[]{:S(2)}, u32[]{:S(2)}) async-start(f32[16,4,2,512]{3,1,2,0:T(4,128)} %copy.86), calls=%async_computation.1 | async-start | bytes 524288 | tf_op jit(solution)/shard_map/all_to_all | solution.py:172
  342.9 8.7 %all-to-all-done.1 = f32[16,4,2,512]{3,1,2,0:T(4,128)S(1)} async-done(((f32[16,4,2,512]{3,1,2,0:T(4,128)}), f32[16,4,2,512]{3,1,2,0:T(4,128)S(1)}, u32[]{:S(2)}, u32[]{:S(2)}) %all-to-all-start.1) | async-done | bytes 262176 | tf_op jit(solution)/shard_map/all_to_all | solution.py:172
  (451 shorter events, 191.8 us)
Async XLA Ops:
  2.3 25.6 %collective-permute-start.3 = (f32[2,2,1,4096]{3,1,2,0:T(2,128)}, f32[2,2,1,4096]{3,1,2,0:T(2,128)}, u32[]{:S(2)}, u32[]{:S(2)}) collective-permute-start(f32[2,2,1,4096]{3,1,2,0:T(2,128)} %pad_maximum_fusion.1), channel_id=1, source_target_pairs={{16,0},{32,16},{48,32},{64,48},{80,64},{96,80},{112,96},{17,1},{33... | collective-permute-start | bytes 196616 | tf_op jit(solution)/shard_map/ppermute | solution.py:16
  4.4 22.1 %collective-permute-start.4 = (f32[2,2,1024]{2,0,1:T(2,128)S(1)}, f32[2,2,1024]{2,0,1:T(2,128)S(1)}, u32[]{:S(2)}, u32[]{:S(2)}) collective-permute-start(f32[2,2,1024]{2,0,1:T(2,128)S(1)} %pad_maximum_fusion.18), channel_id=1, source_target_pairs={{1,0},{2,1},{3,2},{4,3},{5,4},{6,5},{7,6},{8,7},{9,8},{10,9},{11,1... | collective-permute-start | bytes 49160 | tf_op jit(solution)/shard_map/ppermute | solution.py:16
  7.9 23.6 %collective-permute-start = (f32[2,2,1,4096]{3,1,2,0:T(2,128)}, f32[2,2,1,4096]{3,1,2,0:T(2,128)}, u32[]{:S(2)}, u32[]{:S(2)}) collective-permute-start(f32[2,2,1,4096]{3,1,2,0:T(2,128)} %pad_maximum_fusion), channel_id=1, source_target_pairs={{16,0},{32,16},{48,32},{64,48},{80,64},{96,80},{112,96},{17,1},{33... | collective-permute-start | bytes 196616 | tf_op jit(solution)/shard_map/ppermute | solution.py:16
  11.9 15.3 %collective-permute-start.1 = (f32[2,2,1024]{2,0,1:T(2,128)S(1)}, f32[2,2,1024]{2,0,1:T(2,128)S(1)}, u32[]{:S(2)}, u32[]{:S(2)}) collective-permute-start(f32[2,2,1024]{2,0,1:T(2,128)S(1)} %pad_maximum_fusion.16), channel_id=1, source_target_pairs={{1,0},{2,1},{3,2},{4,3},{5,4},{6,5},{7,6},{8,7},{9,8},{10,9},{11,1... | collective-permute-start | bytes 49160 | tf_op jit(solution)/shard_map/ppermute | solution.py:16
  36.8 18.3 %collective-permute-start.5 = (f32[2,2,1024]{2,0,1:T(2,128)}, f32[2,2,1024]{2,0,1:T(2,128)}, u32[]{:S(2)}, u32[]{:S(2)}) collective-permute-start(f32[2,2,1024]{2,0,1:T(2,128)} %pad_maximum_fusion.19), channel_id=1, source_target_pairs={{0,1},{1,2},{2,3},{3,4},{4,5},{5,6},{6,7},{7,8},{8,9},{9,10},{10,1... | collective-permute-start | bytes 49160 | tf_op jit(solution)/shard_map/ppermute | solution.py:16
  43.0 14.2 %collective-permute-start.6 = (f32[2,2,1,4096]{3,1,2,0:T(2,128)}, f32[2,2,1,4096]{3,1,2,0:T(2,128)}, u32[]{:S(2)}, u32[]{:S(2)}) collective-permute-start(f32[2,2,1,4096]{3,1,2,0:T(2,128)} %pad_maximum_fusion.2), channel_id=1, source_target_pairs={{0,16},{16,32},{32,48},{48,64},{64,80},{80,96},{96,112},{1,17},{17... | collective-permute-start | bytes 196616 | tf_op jit(solution)/shard_map/ppermute | solution.py:16
  48.5 14.3 %collective-permute-start.18 = (f32[2,2,1,4096]{3,1,2,0:T(2,128)}, f32[2,2,1,4096]{3,1,2,0:T(2,128)}, u32[]{:S(2)}, u32[]{:S(2)}) collective-permute-start(f32[2,2,1,4096]{3,1,2,0:T(2,128)} %pad_maximum_fusion.8), channel_id=1, source_target_pairs={{0,16},{16,32},{32,48},{48,64},{64,80},{80,96},{96,112},{1,17},{17... | collective-permute-start | bytes 196616 | tf_op jit(solution)/shard_map/ppermute | solution.py:16
  51.8 4.8 %collective-permute-start.2 = (f32[2,2,1024]{2,0,1:T(2,128)S(1)}, f32[2,2,1024]{2,0,1:T(2,128)S(1)}, u32[]{:S(2)}, u32[]{:S(2)}) collective-permute-start(f32[2,2,1024]{2,0,1:T(2,128)S(1)} %pad_maximum_fusion.17), channel_id=1, source_target_pairs={{0,1},{1,2},{2,3},{3,4},{4,5},{5,6},{6,7},{7,8},{8,9},{9,10},{10,1... | collective-permute-start | bytes 49160 | tf_op jit(solution)/shard_map/ppermute | solution.py:16
  61.6 10.5 %collective-permute-start.8 = (f32[2,2,1024]{2,0,1:T(2,128)S(1)}, f32[2,2,1024]{2,0,1:T(2,128)S(1)}, u32[]{:S(2)}, u32[]{:S(2)}) collective-permute-start(f32[2,2,1024]{2,0,1:T(2,128)S(1)} %pad_maximum_fusion.20), channel_id=1, source_target_pairs={{1,0},{2,1},{3,2},{4,3},{5,4},{6,5},{7,6},{8,7},{9,8},{10,9},{11,1... | collective-permute-start | bytes 49160 | tf_op jit(solution)/shard_map/ppermute | solution.py:16
  69.6 4.3 %collective-permute-start.7 = (f32[2,2,1,4096]{3,1,2,0:T(2,128)S(1)}, f32[2,2,1,4096]{3,1,2,0:T(2,128)S(1)}, u32[]{:S(2)}, u32[]{:S(2)}) collective-permute-start(f32[2,2,1,4096]{3,1,2,0:T(2,128)S(1)} %pad_maximum_fusion.3), channel_id=1, source_target_pairs={{16,0},{32,16},{48,32},{64,48},{80,64},{96,80},{112,96},{17,1},{33... | collective-permute-start | bytes 196616 | tf_op jit(solution)/shard_map/ppermute | solution.py:16
  77.7 8.1 %collective-permute-start.9 = (f32[2,2,1024]{2,0,1:T(2,128)S(1)}, f32[2,2,1024]{2,0,1:T(2,128)S(1)}, u32[]{:S(2)}, u32[]{:S(2)}) collective-permute-start(f32[2,2,1024]{2,0,1:T(2,128)S(1)} %pad_maximum_fusion.21), channel_id=1, source_target_pairs={{0,1},{1,2},{2,3},{3,4},{4,5},{5,6},{6,7},{7,8},{8,9},{9,10},{10,1... | collective-permute-start | bytes 49160 | tf_op jit(solution)/shard_map/ppermute | solution.py:16
  82.4 5.6 %collective-permute-start.10 = (f32[2,2,1,4096]{3,1,2,0:T(2,128)S(1)}, f32[2,2,1,4096]{3,1,2,0:T(2,128)S(1)}, u32[]{:S(2)}, u32[]{:S(2)}) collective-permute-start(f32[2,2,1,4096]{3,1,2,0:T(2,128)S(1)} %pad_maximum_fusion.4), channel_id=1, source_target_pairs={{0,16},{16,32},{32,48},{48,64},{64,80},{80,96},{96,112},{1,17},{17... | collective-permute-start | bytes 196616 | tf_op jit(solution)/shard_map/ppermute | solution.py:16
  96.4 10.4 %collective-permute-start.12 = (f32[2,2,1024]{2,0,1:T(2,128)S(1)}, f32[2,2,1024]{2,0,1:T(2,128)}, u32[]{:S(2)}, u32[]{:S(2)}) collective-permute-start(f32[2,2,1024]{2,0,1:T(2,128)S(1)} %pad_maximum_fusion.22), channel_id=1, source_target_pairs={{1,0},{2,1},{3,2},{4,3},{5,4},{6,5},{7,6},{8,7},{9,8},{10,9},{11,1... | collective-permute-start | bytes 49160 | tf_op jit(solution)/shard_map/ppermute | solution.py:16
  105.0 4.1 %collective-permute-start.11 = (f32[2,2,1,4096]{3,1,2,0:T(2,128)}, f32[2,2,1,4096]{3,1,2,0:T(2,128)}, u32[]{:S(2)}, u32[]{:S(2)}) collective-permute-start(f32[2,2,1,4096]{3,1,2,0:T(2,128)} %pad_maximum_fusion.5), channel_id=1, source_target_pairs={{16,0},{32,16},{48,32},{64,48},{80,64},{96,80},{112,96},{17,1},{33... | collective-permute-start | bytes 196616 | tf_op jit(solution)/shard_map/ppermute | solution.py:16
  114.9 9.9 %collective-permute-start.13 = (f32[2,2,1024]{2,0,1:T(2,128)S(1)}, f32[2,2,1024]{2,0,1:T(2,128)S(1)}, u32[]{:S(2)}, u32[]{:S(2)}) collective-permute-start(f32[2,2,1024]{2,0,1:T(2,128)S(1)} %pad_maximum_fusion.23), channel_id=1, source_target_pairs={{0,1},{1,2},{2,3},{3,4},{4,5},{5,6},{6,7},{7,8},{8,9},{9,10},{10,1... | collective-permute-start | bytes 49160 | tf_op jit(solution)/shard_map/ppermute | solution.py:16
  121.1 5.6 %collective-permute-start.14 = (f32[2,2,1,4096]{3,1,2,0:T(2,128)S(1)}, f32[2,2,1,4096]{3,1,2,0:T(2,128)S(1)}, u32[]{:S(2)}, u32[]{:S(2)}) collective-permute-start(f32[2,2,1,4096]{3,1,2,0:T(2,128)S(1)} %pad_maximum_fusion.6), channel_id=1, source_target_pairs={{0,16},{16,32},{32,48},{48,64},{64,80},{80,96},{96,112},{1,17},{17... | collective-permute-start | bytes 196616 | tf_op jit(solution)/shard_map/ppermute | solution.py:16
  136.5 10.6 %collective-permute-start.16 = (f32[2,2,1024]{2,0,1:T(2,128)S(1)}, f32[2,2,1024]{2,0,1:T(2,128)}, u32[]{:S(2)}, u32[]{:S(2)}) collective-permute-start(f32[2,2,1024]{2,0,1:T(2,128)S(1)} %pad_maximum_fusion.24), channel_id=1, source_target_pairs={{1,0},{2,1},{3,2},{4,3},{5,4},{6,5},{7,6},{8,7},{9,8},{10,9},{11,1... | collective-permute-start | bytes 49160 | tf_op jit(solution)/shard_map/ppermute | solution.py:16
  145.2 4.1 %collective-permute-start.15 = (f32[2,2,1,4096]{3,1,2,0:T(2,128)}, f32[2,2,1,4096]{3,1,2,0:T(2,128)}, u32[]{:S(2)}, u32[]{:S(2)}) collective-permute-start(f32[2,2,1,4096]{3,1,2,0:T(2,128)} %pad_maximum_fusion.7), channel_id=1, source_target_pairs={{16,0},{32,16},{48,32},{64,48},{80,64},{96,80},{112,96},{17,1},{33... | collective-permute-start | bytes 196616 | tf_op jit(solution)/shard_map/ppermute | solution.py:16
  158.9 10.6 %collective-permute-start.17 = (f32[2,2,1024]{2,0,1:T(2,128)S(1)}, f32[2,2,1024]{2,0,1:T(2,128)}, u32[]{:S(2)}, u32[]{:S(2)}) collective-permute-start(f32[2,2,1024]{2,0,1:T(2,128)S(1)} %pad_maximum_fusion.25), channel_id=1, source_target_pairs={{0,1},{1,2},{2,3},{3,4},{4,5},{5,6},{6,7},{7,8},{8,9},{9,10},{10,1... | collective-permute-start | bytes 49160 | tf_op jit(solution)/shard_map/ppermute | solution.py:16
  165.8 5.9 %collective-permute-start.19 = (f32[2,2,1,4096]{3,1,2,0:T(2,128)}, f32[2,2,1,4096]{3,1,2,0:T(2,128)}, u32[]{:S(2)}, u32[]{:S(2)}) collective-permute-start(f32[2,2,1,4096]{3,1,2,0:T(2,128)} %pad_maximum_fusion.9), channel_id=1, source_target_pairs={{0,16},{16,32},{32,48},{48,64},{64,80},{80,96},{96,112},{1,17},{17... | collective-permute-start | bytes 196616 | tf_op jit(solution)/shard_map/ppermute | solution.py:16
  180.4 12.9 %collective-permute-start.21 = (f32[2,2,1024]{2,0,1:T(2,128)S(1)}, f32[2,2,1024]{2,0,1:T(2,128)}, u32[]{:S(2)}, u32[]{:S(2)}) collective-permute-start(f32[2,2,1024]{2,0,1:T(2,128)S(1)} %pad_maximum_fusion.26), channel_id=1, source_target_pairs={{1,0},{2,1},{3,2},{4,3},{5,4},{6,5},{7,6},{8,7},{9,8},{10,9},{11,1... | collective-permute-start | bytes 49160 | tf_op jit(solution)/shard_map/ppermute | solution.py:16
  191.4 4.1 %collective-permute-start.20 = (f32[2,2,1,4096]{3,1,2,0:T(2,128)}, f32[2,2,1,4096]{3,1,2,0:T(2,128)S(1)}, u32[]{:S(2)}, u32[]{:S(2)}) collective-permute-start(f32[2,2,1,4096]{3,1,2,0:T(2,128)} %pad_maximum_fusion.10), channel_id=1, source_target_pairs={{16,0},{32,16},{48,32},{64,48},{80,64},{96,80},{112,96},{17,1},{33... | collective-permute-start | bytes 196616 | tf_op jit(solution)/shard_map/ppermute | solution.py:16
  200.9 11.9 %collective-permute-start.22 = (f32[2,2,1024]{2,0,1:T(2,128)S(1)}, f32[2,2,1024]{2,0,1:T(2,128)}, u32[]{:S(2)}, u32[]{:S(2)}) collective-permute-start(f32[2,2,1024]{2,0,1:T(2,128)S(1)} %pad_maximum_fusion.27), channel_id=1, source_target_pairs={{0,1},{1,2},{2,3},{3,4},{4,5},{5,6},{6,7},{7,8},{8,9},{9,10},{10,1... | collective-permute-start | bytes 49160 | tf_op jit(solution)/shard_map/ppermute | solution.py:16
  209.3 5.8 %collective-permute-start.23 = (f32[2,2,1,4096]{3,1,2,0:T(2,128)}, f32[2,2,1,4096]{3,1,2,0:T(2,128)S(1)}, u32[]{:S(2)}, u32[]{:S(2)}) collective-permute-start(f32[2,2,1,4096]{3,1,2,0:T(2,128)} %pad_maximum_fusion.11), channel_id=1, source_target_pairs={{0,16},{16,32},{32,48},{48,64},{64,80},{80,96},{96,112},{1,17},{17... | collective-permute-start | bytes 196616 | tf_op jit(solution)/shard_map/ppermute | solution.py:16
  219.6 13.0 %collective-permute-start.25 = (f32[2,2,1024]{2,0,1:T(2,128)S(1)}, f32[2,2,1024]{2,0,1:T(2,128)}, u32[]{:S(2)}, u32[]{:S(2)}) collective-permute-start(f32[2,2,1024]{2,0,1:T(2,128)S(1)} %pad_maximum_fusion.28), channel_id=1, source_target_pairs={{1,0},{2,1},{3,2},{4,3},{5,4},{6,5},{7,6},{8,7},{9,8},{10,9},{11,1... | collective-permute-start | bytes 49160 | tf_op jit(solution)/shard_map/ppermute | solution.py:16
  230.6 4.1 %collective-permute-start.24 = (f32[2,2,1,4096]{3,1,2,0:T(2,128)}, f32[2,2,1,4096]{3,1,2,0:T(2,128)S(1)}, u32[]{:S(2)}, u32[]{:S(2)}) collective-permute-start(f32[2,2,1,4096]{3,1,2,0:T(2,128)} %pad_maximum_fusion.12), channel_id=1, source_target_pairs={{16,0},{32,16},{48,32},{64,48},{80,64},{96,80},{112,96},{17,1},{33... | collective-permute-start | bytes 196616 | tf_op jit(solution)/shard_map/ppermute | solution.py:16
  240.1 11.9 %collective-permute-start.26 = (f32[2,2,1024]{2,0,1:T(2,128)S(1)}, f32[2,2,1024]{2,0,1:T(2,128)}, u32[]{:S(2)}, u32[]{:S(2)}) collective-permute-start(f32[2,2,1024]{2,0,1:T(2,128)S(1)} %pad_maximum_fusion.29), channel_id=1, source_target_pairs={{0,1},{1,2},{2,3},{3,4},{4,5},{5,6},{6,7},{7,8},{8,9},{9,10},{10,1... | collective-permute-start | bytes 49160 | tf_op jit(solution)/shard_map/ppermute | solution.py:16
  248.5 5.8 %collective-permute-start.27 = (f32[2,2,1,4096]{3,1,2,0:T(2,128)}, f32[2,2,1,4096]{3,1,2,0:T(2,128)S(1)}, u32[]{:S(2)}, u32[]{:S(2)}) collective-permute-start(f32[2,2,1,4096]{3,1,2,0:T(2,128)} %pad_maximum_fusion.13), channel_id=1, source_target_pairs={{0,16},{16,32},{32,48},{48,64},{64,80},{80,96},{96,112},{1,17},{17... | collective-permute-start | bytes 196616 | tf_op jit(solution)/shard_map/ppermute | solution.py:16
  261.0 12.3 %collective-permute-start.29 = (f32[2,2,1024]{2,0,1:T(2,128)S(1)}, f32[2,2,1024]{2,0,1:T(2,128)}, u32[]{:S(2)}, u32[]{:S(2)}) collective-permute-start(f32[2,2,1024]{2,0,1:T(2,128)S(1)} %pad_maximum_fusion.30), channel_id=1, source_target_pairs={{1,0},{2,1},{3,2},{4,3},{5,4},{6,5},{7,6},{8,7},{9,8},{10,9},{11,1... | collective-permute-start | bytes 49160 | tf_op jit(solution)/shard_map/ppermute | solution.py:16
  280.4 10.2 %collective-permute-start.30 = (f32[2,2,1024]{2,0,1:T(2,128)S(1)}, f32[2,2,1024]{2,0,1:T(2,128)S(1)}, u32[]{:S(2)}, u32[]{:S(2)}) collective-permute-start(f32[2,2,1024]{2,0,1:T(2,128)S(1)} %pad_maximum_fusion.31), channel_id=1, source_target_pairs={{0,1},{1,2},{2,3},{3,4},{4,5},{5,6},{6,7},{7,8},{8,9},{9,10},{10,1... | collective-permute-start | bytes 49160 | tf_op jit(solution)/shard_map/ppermute | solution.py:16
  286.6 5.6 %collective-permute-start.31 = (f32[2,2,1,4096]{3,1,2,0:T(2,128)S(1)}, f32[2,2,1,4096]{3,1,2,0:T(2,128)S(1)}, u32[]{:S(2)}, u32[]{:S(2)}) collective-permute-start(f32[2,2,1,4096]{3,1,2,0:T(2,128)S(1)} %pad_maximum_fusion.15), channel_id=1, source_target_pairs={{0,16},{16,32},{32,48},{48,64},{64,80},{80,96},{96,112},{1,17},{17... | collective-permute-start | bytes 196616 | tf_op jit(solution)/shard_map/ppermute | solution.py:16
  327.9 23.7 %all-to-all-start.1 = ((f32[16,4,2,512]{3,1,2,0:T(4,128)}), f32[16,4,2,512]{3,1,2,0:T(4,128)S(1)}, u32[]{:S(2)}, u32[]{:S(2)}) async-start(f32[16,4,2,512]{3,1,2,0:T(4,128)} %copy.86), calls=%async_computation.1 | async-start | bytes 524288 | tf_op jit(solution)/shard_map/all_to_all | solution.py:172
  (74 other events, 567.2 us)
where the time goes:
time: 357 us; the launch traced here: 353 us
  local copies, waits for them, and re-layouts  122 us (34%)
  starting transfers between devices  113 us (32%)
  other arithmetic  71.6 us (20%)
  waiting for transfers between devices  26.9 us (8%)
  blocking collectives  17.4 us (5%)
    ppermute x32, starting transfers between devices, passed_along(): return lax.ppermute(shard, axis, pairs)  98.2 us
    sub x8, other arithmetic, magnetic_update(): magnetic[0]  23.2 us
    slice x16, local copies, waits for them, and re-layouts, upper_y(): return jnp.concatenate([values[..., z_cells:], ghosts], axis=-1)  21.3 us
    ppermute x32, waiting for transfers between devices, passed_along(): return lax.ppermute(shard, axis, pairs)  18.3 us
    all_to_all x1, blocking collectives, per_device(): lax.all_to_all(sectioned, 'src', split_axis=3, concat_axis=2, tiled=True)  17.4 us
    slice x16, local copies, waits for them, and re-layouts, upper_z(): values[..., 1:]  17.2 us
    reduce_sum x3, other arithmetic, per_device(): density = density + jnp.sum(intersection, axis=0)  16 us
    slice x16, local copies, waits for them, and re-layouts, upper_x(): return jnp.concatenate([values[..., 1:, :], ghosts], axis=-2)  15.9 us
  transfers between devices with their start and end apart: 33, of which 14 were waited for; matrix products, arithmetic and copies ran while one was open for 27% of the time, Pallas kernels for 0%

commit v1 on v0

--- a/solution.py
+++ b/solution.py
@@ -2,6 +2,7 @@
 import jax.numpy as jnp
 from jax import lax
 from jax.sharding import PartitionSpec as P
+from jax.lax import all_to_all, axis_size
 
 NZ = 64
 STEPS = 4
@@ -169,8 +170,17 @@
         .set(blocks, mode="drop")
     )
     sectioned = outgoing.reshape(peers, capacity, 1, -1)
+
+    def watch_desk(message, comm_axis, at_axis, dimension_no):
+        q_next = axis_size(comm_axis)
+        local_part = jnp.split(message, q_next, axis=at_axis)
+        new = jnp.stack(local_part)
+        x_now = all_to_all(new, axis_name=comm_axis, split_axis=0, concat_axis=0)
+        block_last = jnp.concatenate(x_now, axis=dimension_no)
+        return block_last
+
     arrived = lax.all_to_all(
-        lax.all_to_all(sectioned, "src", split_axis=3, concat_axis=2, tiled=True),
+        watch_desk(sectioned, "src", at_axis=3, dimension_no=2),
         "gy",
         split_axis=0,
         concat_axis=0,

time: 357 us -> 353 us (0.989)
    unnamed x148 -> x178, local copies, waits for them, and re-layouts: 15 us -> 11.8 us
where the time goes in v1:
time: 353 us; the launch traced here: 349 us
  local copies, waits for them, and re-layouts  120 us (34%)
  starting transfers between devices  113 us (32%)
  other arithmetic  69.5 us (20%)
  waiting for transfers between devices  27.6 us (8%)
  blocking collectives  17.4 us (5%)
    ppermute x32, starting transfers between devices, passed_along(): return lax.ppermute(shard, axis, pairs)  98.2 us
    sub x8, other arithmetic, magnetic_update(): magnetic[0]  24.1 us
    slice x16, local copies, waits for them, and re-layouts, upper_y(): return jnp.concatenate([values[..., z_cells:], ghosts], axis=-1)  22.5 us
    ppermute x32, waiting for transfers between devices, passed_along(): return lax.ppermute(shard, axis, pairs)  19 us
    slice x16, local copies, waits for them, and re-layouts, upper_z(): values[..., 1:]  18.3 us
    slice x16, local copies, waits for them, and re-layouts, upper_x(): return jnp.concatenate([values[..., 1:, :], ghosts], axis=-2)  17.9 us
    all_to_all x1, blocking collectives, watch_desk(): x_now = all_to_all(new, axis_name=comm_axis, split_axis=0, concat_axis=0)  17.4 us
    reduce_sum x3, other arithmetic, per_device(): density = density + jnp.sum(intersection, axis=0)  16.5 us
  transfers between devices with their start and end apart: 33, of which 14 were waited for; matrix products, arithmetic and copies ran while one was open for 27% of the time, Pallas kernels for 0%

profile of v1, /device:TPU:32, one launch (start us, length us, event | category | flops | bytes accessed | tf_op | source)
XLA Modules:
  0.0 349.3 jit_solution(14620851322780358808)
XLA Ops:
  0.0 2.4 slice_bitcast_fusion.2
  10.6 3.8 %collective-permute-start = (f32[2,2,1,4096]{3,1,2,0:T(2,128)}, f32[2,2,1,4096]{3,1,2,0:T(2,128)}, u32[]{:S(2)}, u32[]{:S(2)}) collective-permute-start(f32[2,2,1,4096]{3,1,2,0:T(2,128)} %pad_maximum_fusion.1), channel_id=1, source_target_pairs={{16,0},{32,16},{48,32},{64,48},{80,64},{96,80},{112,96},{17,1},{33... | collective-permute-start | bytes 196616 | tf_op jit(solution)/shard_map/ppermute | solution.py:17
  44.7 4.9 %collective-permute-start.5 = (f32[2,2,1024]{2,0,1:T(2,128)S(1)}, f32[2,2,1024]{2,0,1:T(2,128)S(1)}, u32[]{:S(2)}, u32[]{:S(2)}) collective-permute-start(f32[2,2,1024]{2,0,1:T(2,128)S(1)} %pad_maximum_fusion.20), channel_id=1, source_target_pairs={{0,1},{1,2},{2,3},{3,4},{4,5},{5,6},{6,7},{7,8},{8,9},{9,10},{10,1... | collective-permute-start | bytes 49160 | tf_op jit(solution)/shard_map/ppermute | solution.py:17
  52.6 2.8 fusion.102
  56.1 2.3 collective-permute-start.18
  58.7 3.9 %collective-permute-start.2 = (f32[2,2,1024]{2,0,1:T(2,128)S(1)}, f32[2,2,1024]{2,0,1:T(2,128)S(1)}, u32[]{:S(2)}, u32[]{:S(2)}) collective-permute-start(f32[2,2,1024]{2,0,1:T(2,128)S(1)} %pad_maximum_fusion.18), channel_id=1, source_target_pairs={{0,1},{1,2},{2,3},{3,4},{4,5},{5,6},{6,7},{7,8},{8,9},{9,10},{10,1... | collective-permute-start | bytes 49160 | tf_op jit(solution)/shard_map/ppermute | solution.py:17
  76.2 2.4 collective-permute-start.7
  80.6 2.5 fusion.118
  84.3 4.5 %collective-permute-start.9 = (f32[2,2,1024]{2,0,1:T(2,128)S(1)}, f32[2,2,1024]{2,0,1:T(2,128)S(1)}, u32[]{:S(2)}, u32[]{:S(2)}) collective-permute-start(f32[2,2,1024]{2,0,1:T(2,128)S(1)} %pad_maximum_fusion.22), channel_id=1, source_target_pairs={{0,1},{1,2},{2,3},{3,4},{4,5},{5,6},{6,7},{7,8},{8,9},{9,10},{10,1... | collective-permute-start | bytes 49160 | tf_op jit(solution)/shard_map/ppermute | solution.py:17
  88.9 3.5 %collective-permute-start.10 = (f32[2,2,1,4096]{3,1,2,0:T(2,128)S(1)}, f32[2,2,1,4096]{3,1,2,0:T(2,128)S(1)}, u32[]{:S(2)}, u32[]{:S(2)}) collective-permute-start(f32[2,2,1,4096]{3,1,2,0:T(2,128)S(1)} %pad_maximum_fusion.5), channel_id=1, source_target_pairs={{0,16},{16,32},{32,48},{48,64},{64,80},{80,96},{96,112},{1,17},{17... | collective-permute-start | bytes 196616 | tf_op jit(solution)/shard_map/ppermute | solution.py:17
  116.6 3.7 %fusion.126 = (f32[2,16,4096]{2,1,0:T(8,128)S(1)}, f32[2,16,4096]{2,1,0:T(8,128)}, f32[2,16,4096]{2,1,0:T(8,128)S(1)}) fusion(f32[2,16,4096]{2,1,0:T(8,128)} %copy-done.12, f32[2,16,4096]{2,1,0:T(8,128)S(1)} %get-tuple-element.36, f32[2,16,4096]{2,1,0:T(8,128)S(1)} %fusion.184, f32[2,16,64]{2,1,0:T(8,128)S(1)} %get-tuple-element.112, ...), kind=kLoop, calls=%fused_computation.132 | loop fusion | flops 3014656 | bytes 7900928 | tf_op jit(solution)/shard_map/sub | solution.py:49
  121.5 5.1 %collective-permute-start.13 = (f32[2,2,1024]{2,0,1:T(2,128)S(1)}, f32[2,2,1024]{2,0,1:T(2,128)S(1)}, u32[]{:S(2)}, u32[]{:S(2)}) collective-permute-start(f32[2,2,1024]{2,0,1:T(2,128)S(1)} %pad_maximum_fusion.24), channel_id=1, source_target_pairs={{0,1},{1,2},{2,3},{3,4},{4,5},{5,6},{6,7},{7,8},{8,9},{9,10},{10,1... | collective-permute-start | bytes 49160 | tf_op jit(solution)/shard_map/ppermute | solution.py:17
  127.7 3.7 %collective-permute-start.14 = (f32[2,2,1,4096]{3,1,2,0:T(2,128)S(1)}, f32[2,2,1,4096]{3,1,2,0:T(2,128)S(1)}, u32[]{:S(2)}, u32[]{:S(2)}) collective-permute-start(f32[2,2,1,4096]{3,1,2,0:T(2,128)S(1)} %pad_maximum_fusion.7), channel_id=1, source_target_pairs={{0,16},{16,32},{32,48},{48,64},{64,80},{80,96},{96,112},{1,17},{17... | collective-permute-start | bytes 196616 | tf_op jit(solution)/shard_map/ppermute | solution.py:17
  135.9 2.3 fusion.59
  156.9 3.0 fusion.134
  165.6 5.4 %collective-permute-start.17 = (f32[2,2,1024]{2,0,1:T(2,128)S(1)}, f32[2,2,1024]{2,0,1:T(2,128)}, u32[]{:S(2)}, u32[]{:S(2)}) collective-permute-start(f32[2,2,1024]{2,0,1:T(2,128)S(1)} %pad_maximum_fusion.26), channel_id=1, source_target_pairs={{0,1},{1,2},{2,3},{3,4},{4,5},{5,6},{6,7},{7,8},{8,9},{9,10},{10,1... | collective-permute-start | bytes 49160 | tf_op jit(solution)/shard_map/ppermute | solution.py:17
  172.5 3.7 %collective-permute-start.19 = (f32[2,2,1,4096]{3,1,2,0:T(2,128)}, f32[2,2,1,4096]{3,1,2,0:T(2,128)}, u32[]{:S(2)}, u32[]{:S(2)}) collective-permute-start(f32[2,2,1,4096]{3,1,2,0:T(2,128)} %pad_maximum_fusion.10), channel_id=1, source_target_pairs={{0,16},{16,32},{32,48},{48,64},{64,80},{80,96},{96,112},{1,17},{17... | collective-permute-start | bytes 196616 | tf_op jit(solution)/shard_map/ppermute | solution.py:17
  179.3 6.6 %fusion.166 = (f32[16,4096]{1,0:T(8,128)}, f32[2,16,4096]{2,1,0:T(8,128)S(1)}, f32[2,16,4096]{2,1,0:T(8,128)S(1)}, f32[2,16,4096]{2,1,0:T(8,128)S(1)}) fusion(f32[2,16,4096]{2,1,0:T(8,128)} %get-tuple-element.35, f32[2,16,4096]{2,1,0:T(8,128)} %copy-done.53, f32[2,16,4096]{2,1,0:T(8,128)S(1)} %get-tuple-element.34, f32[2,16,4096]{2,1,0:T(8,128)} %copy-done.55, ...), kind=kLoop, calls=%fused_computation.172 | loop fusion | flops 7536640 | bytes 14716440 | tf_op jit(solution)/shard_map/reduce_sum | solution.py:154
  202.5 4.1 %fusion.142 = (f32[2,16,4096]{2,1,0:T(8,128)S(1)}, f32[2,16,4096]{2,1,0:T(8,128)}, f32[2,16,4096]{2,1,0:T(8,128)S(1)}) fusion(f32[2,16,4096]{2,1,0:T(8,128)} %copy-done.42, f32[2,16,4096]{2,1,0:T(8,128)} %copy-done.38, f32[2,16,4096]{2,1,0:T(8,128)} %copy-done.24, f32[2,16,64]{2,1,0:T(8,128)S(1)} %get-tuple-element.100, f32[2,16,4032]{2,1,0:T(8,128)} %slice.1120, ...), kind=kLoop, calls=%fused_computation.148 | loop fusion | flops 3014656 | bytes 7900928 | tf_op jit(solution)/shard_map/sub | solution.py:49
  207.8 6.7 %collective-permute-start.22 = (f32[2,2,1024]{2,0,1:T(2,128)S(1)}, f32[2,2,1024]{2,0,1:T(2,128)}, u32[]{:S(2)}, u32[]{:S(2)}) collective-permute-start(f32[2,2,1024]{2,0,1:T(2,128)S(1)} %pad_maximum_fusion.28), channel_id=1, source_target_pairs={{0,1},{1,2},{2,3},{3,4},{4,5},{5,6},{6,7},{7,8},{8,9},{9,10},{10,1... | collective-permute-start | bytes 49160 | tf_op jit(solution)/shard_map/ppermute | solution.py:17
  216.2 3.6 %collective-permute-start.23 = (f32[2,2,1,4096]{3,1,2,0:T(2,128)}, f32[2,2,1,4096]{3,1,2,0:T(2,128)S(1)}, u32[]{:S(2)}, u32[]{:S(2)}) collective-permute-start(f32[2,2,1,4096]{3,1,2,0:T(2,128)} %pad_maximum_fusion.12), channel_id=1, source_target_pairs={{0,16},{16,32},{32,48},{48,64},{64,80},{80,96},{96,112},{1,17},{17... | collective-permute-start | bytes 196616 | tf_op jit(solution)/shard_map/ppermute | solution.py:17
  241.7 4.1 %fusion.150 = (f32[2,16,4096]{2,1,0:T(8,128)S(1)}, f32[2,16,4096]{2,1,0:T(8,128)}, f32[2,16,4096]{2,1,0:T(8,128)S(1)}) fusion(f32[2,16,4096]{2,1,0:T(8,128)} %copy-done.10, f32[2,16,4096]{2,1,0:T(8,128)} %copy-done.41, f32[2,16,4096]{2,1,0:T(8,128)} %copy-done.22, f32[2,16,64]{2,1,0:T(8,128)S(1)} %get-tuple-element.96, f32[2,16,4032]{2,1,0:T(8,128)} %slice.1148, ...), kind=kLoop, calls=%fused_computation.156 | loop fusion | flops 3014656 | bytes 7900928 | tf_op jit(solution)/shard_map/sub | solution.py:49
  247.0 6.7 %collective-permute-start.26 = (f32[2,2,1024]{2,0,1:T(2,128)S(1)}, f32[2,2,1024]{2,0,1:T(2,128)}, u32[]{:S(2)}, u32[]{:S(2)}) collective-permute-start(f32[2,2,1024]{2,0,1:T(2,128)S(1)} %pad_maximum_fusion.30), channel_id=1, source_target_pairs={{0,1},{1,2},{2,3},{3,4},{4,5},{5,6},{6,7},{7,8},{8,9},{9,10},{10,1... | collective-permute-start | bytes 49160 | tf_op jit(solution)/shard_map/ppermute | solution.py:17
  255.4 3.6 %collective-permute-start.27 = (f32[2,2,1,4096]{3,1,2,0:T(2,128)}, f32[2,2,1,4096]{3,1,2,0:T(2,128)S(1)}, u32[]{:S(2)}, u32[]{:S(2)}) collective-permute-start(f32[2,2,1,4096]{3,1,2,0:T(2,128)} %pad_maximum_fusion.14), channel_id=1, source_target_pairs={{0,16},{16,32},{32,48},{48,64},{64,80},{80,96},{96,112},{1,17},{17... | collective-permute-start | bytes 196616 | tf_op jit(solution)/shard_map/ppermute | solution.py:17
  261.2 5.6 %add_reduce_fusion.1 = (f32[16,4096]{1,0:T(8,128)}, f32[16,4096]{1,0:T(8,128)}, f32[2,16,4096]{2,1,0:T(8,128)S(1)}, f32[2,16,4096]{2,1,0:T(8,128)S(1)}, f32[2,16,4096]{2,1,0:T(8,128)S(1)}) fusion(f32[2,16,4096]{2,1,0:T(8,128)} %copy-done.22, f32[2,16,4096]{2,1,0:T(8,128)S(1)} %fusion.191, f32[2,16,4096]{2,1,0:T(8,128)S(1)} %fusion.184, ...), kind=kLoop, calls=%fused_computation.295 | loop fusion | flops 5242880 | bytes 13405952 | tf_op jit(solution)/shard_map/reduce_sum | solution.py:154
  283.4 2.8 fusion.158
  287.7 6.1 %collective-permute-start.30 = (f32[2,2,1024]{2,0,1:T(2,128)S(1)}, f32[2,2,1024]{2,0,1:T(2,128)S(1)}, u32[]{:S(2)}, u32[]{:S(2)}) collective-permute-start(f32[2,2,1024]{2,0,1:T(2,128)S(1)} %pad_maximum_fusion.32), channel_id=1, source_target_pairs={{0,1},{1,2},{2,3},{3,4},{4,5},{5,6},{6,7},{7,8},{8,9},{9,10},{10,1... | collective-permute-start | bytes 49160 | tf_op jit(solution)/shard_map/ppermute | solution.py:17
  293.8 4.0 %collective-permute-start.31 = (f32[2,2,1,4096]{3,1,2,0:T(2,128)S(1)}, f32[2,2,1,4096]{3,1,2,0:T(2,128)S(1)}, u32[]{:S(2)}, u32[]{:S(2)}) collective-permute-start(f32[2,2,1,4096]{3,1,2,0:T(2,128)S(1)} %pad_maximum_fusion.16), channel_id=1, source_target_pairs={{0,16},{16,32},{32,48},{48,64},{64,80},{80,96},{96,112},{1,17},{17... | collective-permute-start | bytes 196616 | tf_op jit(solution)/shard_map/ppermute | solution.py:17
  299.5 4.2 %fusion.93 = f32[16,4096]{1,0:T(8,128)S(1)} fusion(f32[2,16,4096]{2,1,0:T(8,128)} %copy-done.44, f32[2,16,4096]{2,1,0:T(8,128)} %copy-done.54, f32[2,16,4096]{2,1,0:T(8,128)} %copy-done.36, f32[2,16,4096]{2,1,0:T(8,128)} %copy-done.56, f32[2,16,4096]{2,1,0:T(8,128)} %copy-done.52, f32[2,16,4032]{2,1,0:T(8,128)} %bitcast.417, ...), kind=kLoop, calls=%fused_computation.99 | loop fusion | flops 4128768 | bytes 9998080 | tf_op jit(solution)/shard_map/reduce_sum | solution.py:154
  306.0 17.4 %all_to_all.10 = f32[2,16,4,1,512]{4,2,1,3,0:T(4,128)S(1)} all-to-all(f32[2,16,4,1,512]{4,2,1,3,0:T(4,128)S(1)} %pad_maximum_fusion), channel_id=1, replica_groups=mesh['src'=2,'gx'=8,'gy'=16] {'src'}, dimensions={0} | all-to-all | bytes 524288 | tf_op jit(solution)/shard_map/all_to_all | solution.py:178
  324.1 15.0 %all-to-all-start.1 = ((f32[16,4,2,512]{3,1,2,0:T(4,128)}), f32[16,4,2,512]{3,1,2,0:T(4,128)S(1)}, u32[]{:S(2)}, u32[]{:S(2)}) async-start(f32[16,4,2,512]{3,1,2,0:T(4,128)} %copy.57), calls=%async_computation.1 | async-start | bytes 524288 | tf_op jit(solution)/shard_map/all_to_all | solution.py:182
  339.1 8.7 %all-to-all-done.1 = f32[16,4,2,512]{3,1,2,0:T(4,128)S(1)} async-done(((f32[16,4,2,512]{3,1,2,0:T(4,128)}), f32[16,4,2,512]{3,1,2,0:T(4,128)S(1)}, u32[]{:S(2)}, u32[]{:S(2)}) %all-to-all-start.1) | async-done | bytes 262176 | tf_op jit(solution)/shard_map/all_to_all | solution.py:182
  (480 shorter events, 188.5 us)
Async XLA Ops:
  4.0 30.5 %collective-permute-start.3 = (f32[2,2,1,4096]{3,1,2,0:T(2,128)}, f32[2,2,1,4096]{3,1,2,0:T(2,128)}, u32[]{:S(2)}, u32[]{:S(2)}) collective-permute-start(f32[2,2,1,4096]{3,1,2,0:T(2,128)} %pad_maximum_fusion.2), channel_id=1, source_target_pairs={{16,0},{32,16},{48,32},{64,48},{80,64},{96,80},{112,96},{17,1},{33... | collective-permute-start | bytes 196616 | tf_op jit(solution)/shard_map/ppermute | solution.py:17
  6.8 26.3 %collective-permute-start.4 = (f32[2,2,1024]{2,0,1:T(2,128)S(1)}, f32[2,2,1024]{2,0,1:T(2,128)S(1)}, u32[]{:S(2)}, u32[]{:S(2)}) collective-permute-start(f32[2,2,1024]{2,0,1:T(2,128)S(1)} %pad_maximum_fusion.19), channel_id=1, source_target_pairs={{1,0},{2,1},{3,2},{4,3},{5,4},{6,5},{7,6},{8,7},{9,8},{10,9},{11,1... | collective-permute-start | bytes 49160 | tf_op jit(solution)/shard_map/ppermute | solution.py:17
  10.6 27.7 %collective-permute-start = (f32[2,2,1,4096]{3,1,2,0:T(2,128)}, f32[2,2,1,4096]{3,1,2,0:T(2,128)}, u32[]{:S(2)}, u32[]{:S(2)}) collective-permute-start(f32[2,2,1,4096]{3,1,2,0:T(2,128)} %pad_maximum_fusion.1), channel_id=1, source_target_pairs={{16,0},{32,16},{48,32},{64,48},{80,64},{96,80},{112,96},{17,1},{33... | collective-permute-start | bytes 196616 | tf_op jit(solution)/shard_map/ppermute | solution.py:17
  15.3 18.5 %collective-permute-start.1 = (f32[2,2,1024]{2,0,1:T(2,128)S(1)}, f32[2,2,1024]{2,0,1:T(2,128)S(1)}, u32[]{:S(2)}, u32[]{:S(2)}) collective-permute-start(f32[2,2,1024]{2,0,1:T(2,128)S(1)} %pad_maximum_fusion.17), channel_id=1, source_target_pairs={{1,0},{2,1},{3,2},{4,3},{5,4},{6,5},{7,6},{8,7},{9,8},{10,9},{11,1... | collective-permute-start | bytes 49160 | tf_op jit(solution)/shard_map/ppermute | solution.py:17
  44.7 17.9 %collective-permute-start.5 = (f32[2,2,1024]{2,0,1:T(2,128)S(1)}, f32[2,2,1024]{2,0,1:T(2,128)S(1)}, u32[]{:S(2)}, u32[]{:S(2)}) collective-permute-start(f32[2,2,1024]{2,0,1:T(2,128)S(1)} %pad_maximum_fusion.20), channel_id=1, source_target_pairs={{0,1},{1,2},{2,3},{3,4},{4,5},{5,6},{6,7},{7,8},{8,9},{9,10},{10,1... | collective-permute-start | bytes 49160 | tf_op jit(solution)/shard_map/ppermute | solution.py:17
  50.6 14.1 %collective-permute-start.6 = (f32[2,2,1,4096]{3,1,2,0:T(2,128)S(1)}, f32[2,2,1,4096]{3,1,2,0:T(2,128)S(1)}, u32[]{:S(2)}, u32[]{:S(2)}) collective-permute-start(f32[2,2,1,4096]{3,1,2,0:T(2,128)S(1)} %pad_maximum_fusion.3), channel_id=1, source_target_pairs={{0,16},{16,32},{32,48},{48,64},{64,80},{80,96},{96,112},{1,17},{17... | collective-permute-start | bytes 196616 | tf_op jit(solution)/shard_map/ppermute | solution.py:17
  56.1 13.3 %collective-permute-start.18 = (f32[2,2,1,4096]{3,1,2,0:T(2,128)}, f32[2,2,1,4096]{3,1,2,0:T(2,128)}, u32[]{:S(2)}, u32[]{:S(2)}) collective-permute-start(f32[2,2,1,4096]{3,1,2,0:T(2,128)} %pad_maximum_fusion.9), channel_id=1, source_target_pairs={{0,16},{16,32},{32,48},{48,64},{64,80},{80,96},{96,112},{1,17},{17... | collective-permute-start | bytes 196616 | tf_op jit(solution)/shard_map/ppermute | solution.py:17
  58.7 5.4 %collective-permute-start.2 = (f32[2,2,1024]{2,0,1:T(2,128)S(1)}, f32[2,2,1024]{2,0,1:T(2,128)S(1)}, u32[]{:S(2)}, u32[]{:S(2)}) collective-permute-start(f32[2,2,1024]{2,0,1:T(2,128)S(1)} %pad_maximum_fusion.18), channel_id=1, source_target_pairs={{0,1},{1,2},{2,3},{3,4},{4,5},{5,6},{6,7},{7,8},{8,9},{9,10},{10,1... | collective-permute-start | bytes 49160 | tf_op jit(solution)/shard_map/ppermute | solution.py:17
  68.1 10.5 %collective-permute-start.8 = (f32[2,2,1024]{2,0,1:T(2,128)S(1)}, f32[2,2,1024]{2,0,1:T(2,128)S(1)}, u32[]{:S(2)}, u32[]{:S(2)}) collective-permute-start(f32[2,2,1024]{2,0,1:T(2,128)S(1)} %pad_maximum_fusion.21), channel_id=1, source_target_pairs={{1,0},{2,1},{3,2},{4,3},{5,4},{6,5},{7,6},{8,7},{9,8},{10,9},{11,1... | collective-permute-start | bytes 49160 | tf_op jit(solution)/shard_map/ppermute | solution.py:17
  76.2 4.3 %collective-permute-start.7 = (f32[2,2,1,4096]{3,1,2,0:T(2,128)S(1)}, f32[2,2,1,4096]{3,1,2,0:T(2,128)S(1)}, u32[]{:S(2)}, u32[]{:S(2)}) collective-permute-start(f32[2,2,1,4096]{3,1,2,0:T(2,128)S(1)} %pad_maximum_fusion.4), channel_id=1, source_target_pairs={{16,0},{32,16},{48,32},{64,48},{80,64},{96,80},{112,96},{17,1},{33... | collective-permute-start | bytes 196616 | tf_op jit(solution)/shard_map/ppermute | solution.py:17
  84.3 8.2 %collective-permute-start.9 = (f32[2,2,1024]{2,0,1:T(2,128)S(1)}, f32[2,2,1024]{2,0,1:T(2,128)S(1)}, u32[]{:S(2)}, u32[]{:S(2)}) collective-permute-start(f32[2,2,1024]{2,0,1:T(2,128)S(1)} %pad_maximum_fusion.22), channel_id=1, source_target_pairs={{0,1},{1,2},{2,3},{3,4},{4,5},{5,6},{6,7},{7,8},{8,9},{9,10},{10,1... | collective-permute-start | bytes 49160 | tf_op jit(solution)/shard_map/ppermute | solution.py:17
  88.9 5.6 %collective-permute-start.10 = (f32[2,2,1,4096]{3,1,2,0:T(2,128)S(1)}, f32[2,2,1,4096]{3,1,2,0:T(2,128)S(1)}, u32[]{:S(2)}, u32[]{:S(2)}) collective-permute-start(f32[2,2,1,4096]{3,1,2,0:T(2,128)S(1)} %pad_maximum_fusion.5), channel_id=1, source_target_pairs={{0,16},{16,32},{32,48},{48,64},{64,80},{80,96},{96,112},{1,17},{17... | collective-permute-start | bytes 196616 | tf_op jit(solution)/shard_map/ppermute | solution.py:17
  103.0 10.5 %collective-permute-start.12 = (f32[2,2,1024]{2,0,1:T(2,128)S(1)}, f32[2,2,1024]{2,0,1:T(2,128)}, u32[]{:S(2)}, u32[]{:S(2)}) collective-permute-start(f32[2,2,1024]{2,0,1:T(2,128)S(1)} %pad_maximum_fusion.23), channel_id=1, source_target_pairs={{1,0},{2,1},{3,2},{4,3},{5,4},{6,5},{7,6},{8,7},{9,8},{10,9},{11,1... | collective-permute-start | bytes 49160 | tf_op jit(solution)/shard_map/ppermute | solution.py:17
  111.5 4.1 %collective-permute-start.11 = (f32[2,2,1,4096]{3,1,2,0:T(2,128)}, f32[2,2,1,4096]{3,1,2,0:T(2,128)}, u32[]{:S(2)}, u32[]{:S(2)}) collective-permute-start(f32[2,2,1,4096]{3,1,2,0:T(2,128)} %pad_maximum_fusion.6), channel_id=1, source_target_pairs={{16,0},{32,16},{48,32},{64,48},{80,64},{96,80},{112,96},{17,1},{33... | collective-permute-start | bytes 196616 | tf_op jit(solution)/shard_map/ppermute | solution.py:17
  121.5 9.9 %collective-permute-start.13 = (f32[2,2,1024]{2,0,1:T(2,128)S(1)}, f32[2,2,1024]{2,0,1:T(2,128)S(1)}, u32[]{:S(2)}, u32[]{:S(2)}) collective-permute-start(f32[2,2,1024]{2,0,1:T(2,128)S(1)} %pad_maximum_fusion.24), channel_id=1, source_target_pairs={{0,1},{1,2},{2,3},{3,4},{4,5},{5,6},{6,7},{7,8},{8,9},{9,10},{10,1... | collective-permute-start | bytes 49160 | tf_op jit(solution)/shard_map/ppermute | solution.py:17
  127.7 5.6 %collective-permute-start.14 = (f32[2,2,1,4096]{3,1,2,0:T(2,128)S(1)}, f32[2,2,1,4096]{3,1,2,0:T(2,128)S(1)}, u32[]{:S(2)}, u32[]{:S(2)}) collective-permute-start(f32[2,2,1,4096]{3,1,2,0:T(2,128)S(1)} %pad_maximum_fusion.7), channel_id=1, source_target_pairs={{0,16},{16,32},{32,48},{48,64},{64,80},{80,96},{96,112},{1,17},{17... | collective-permute-start | bytes 196616 | tf_op jit(solution)/shard_map/ppermute | solution.py:17
  143.1 10.6 %collective-permute-start.16 = (f32[2,2,1024]{2,0,1:T(2,128)S(1)}, f32[2,2,1024]{2,0,1:T(2,128)}, u32[]{:S(2)}, u32[]{:S(2)}) collective-permute-start(f32[2,2,1024]{2,0,1:T(2,128)S(1)} %pad_maximum_fusion.25), channel_id=1, source_target_pairs={{1,0},{2,1},{3,2},{4,3},{5,4},{6,5},{7,6},{8,7},{9,8},{10,9},{11,1... | collective-permute-start | bytes 49160 | tf_op jit(solution)/shard_map/ppermute | solution.py:17
  151.8 4.1 %collective-permute-start.15 = (f32[2,2,1,4096]{3,1,2,0:T(2,128)}, f32[2,2,1,4096]{3,1,2,0:T(2,128)}, u32[]{:S(2)}, u32[]{:S(2)}) collective-permute-start(f32[2,2,1,4096]{3,1,2,0:T(2,128)} %pad_maximum_fusion.8), channel_id=1, source_target_pairs={{16,0},{32,16},{48,32},{64,48},{80,64},{96,80},{112,96},{17,1},{33... | collective-permute-start | bytes 196616 | tf_op jit(solution)/shard_map/ppermute | solution.py:17
  165.6 10.6 %collective-permute-start.17 = (f32[2,2,1024]{2,0,1:T(2,128)S(1)}, f32[2,2,1024]{2,0,1:T(2,128)}, u32[]{:S(2)}, u32[]{:S(2)}) collective-permute-start(f32[2,2,1024]{2,0,1:T(2,128)S(1)} %pad_maximum_fusion.26), channel_id=1, source_target_pairs={{0,1},{1,2},{2,3},{3,4},{4,5},{5,6},{6,7},{7,8},{8,9},{9,10},{10,1... | collective-permute-start | bytes 49160 | tf_op jit(solution)/shard_map/ppermute | solution.py:17
  172.5 5.9 %collective-permute-start.19 = (f32[2,2,1,4096]{3,1,2,0:T(2,128)}, f32[2,2,1,4096]{3,1,2,0:T(2,128)}, u32[]{:S(2)}, u32[]{:S(2)}) collective-permute-start(f32[2,2,1,4096]{3,1,2,0:T(2,128)} %pad_maximum_fusion.10), channel_id=1, source_target_pairs={{0,16},{16,32},{32,48},{48,64},{64,80},{80,96},{96,112},{1,17},{17... | collective-permute-start | bytes 196616 | tf_op jit(solution)/shard_map/ppermute | solution.py:17
  187.3 13.0 %collective-permute-start.21 = (f32[2,2,1024]{2,0,1:T(2,128)S(1)}, f32[2,2,1024]{2,0,1:T(2,128)}, u32[]{:S(2)}, u32[]{:S(2)}) collective-permute-start(f32[2,2,1024]{2,0,1:T(2,128)S(1)} %pad_maximum_fusion.27), channel_id=1, source_target_pairs={{1,0},{2,1},{3,2},{4,3},{5,4},{6,5},{7,6},{8,7},{9,8},{10,9},{11,1... | collective-permute-start | bytes 49160 | tf_op jit(solution)/shard_map/ppermute | solution.py:17
  198.3 4.1 %collective-permute-start.20 = (f32[2,2,1,4096]{3,1,2,0:T(2,128)}, f32[2,2,1,4096]{3,1,2,0:T(2,128)S(1)}, u32[]{:S(2)}, u32[]{:S(2)}) collective-permute-start(f32[2,2,1,4096]{3,1,2,0:T(2,128)} %pad_maximum_fusion.11), channel_id=1, source_target_pairs={{16,0},{32,16},{48,32},{64,48},{80,64},{96,80},{112,96},{17,1},{33... | collective-permute-start | bytes 196616 | tf_op jit(solution)/shard_map/ppermute | solution.py:17
  207.8 11.9 %collective-permute-start.22 = (f32[2,2,1024]{2,0,1:T(2,128)S(1)}, f32[2,2,1024]{2,0,1:T(2,128)}, u32[]{:S(2)}, u32[]{:S(2)}) collective-permute-start(f32[2,2,1024]{2,0,1:T(2,128)S(1)} %pad_maximum_fusion.28), channel_id=1, source_target_pairs={{0,1},{1,2},{2,3},{3,4},{4,5},{5,6},{6,7},{7,8},{8,9},{9,10},{10,1... | collective-permute-start | bytes 49160 | tf_op jit(solution)/shard_map/ppermute | solution.py:17
  216.2 5.8 %collective-permute-start.23 = (f32[2,2,1,4096]{3,1,2,0:T(2,128)}, f32[2,2,1,4096]{3,1,2,0:T(2,128)S(1)}, u32[]{:S(2)}, u32[]{:S(2)}) collective-permute-start(f32[2,2,1,4096]{3,1,2,0:T(2,128)} %pad_maximum_fusion.12), channel_id=1, source_target_pairs={{0,16},{16,32},{32,48},{48,64},{64,80},{80,96},{96,112},{1,17},{17... | collective-permute-start | bytes 196616 | tf_op jit(solution)/shard_map/ppermute | solution.py:17
  226.5 12.9 %collective-permute-start.25 = (f32[2,2,1024]{2,0,1:T(2,128)S(1)}, f32[2,2,1024]{2,0,1:T(2,128)}, u32[]{:S(2)}, u32[]{:S(2)}) collective-permute-start(f32[2,2,1024]{2,0,1:T(2,128)S(1)} %pad_maximum_fusion.29), channel_id=1, source_target_pairs={{1,0},{2,1},{3,2},{4,3},{5,4},{6,5},{7,6},{8,7},{9,8},{10,9},{11,1... | collective-permute-start | bytes 49160 | tf_op jit(solution)/shard_map/ppermute | solution.py:17
  237.5 4.1 %collective-permute-start.24 = (f32[2,2,1,4096]{3,1,2,0:T(2,128)}, f32[2,2,1,4096]{3,1,2,0:T(2,128)S(1)}, u32[]{:S(2)}, u32[]{:S(2)}) collective-permute-start(f32[2,2,1,4096]{3,1,2,0:T(2,128)} %pad_maximum_fusion.13), channel_id=1, source_target_pairs={{16,0},{32,16},{48,32},{64,48},{80,64},{96,80},{112,96},{17,1},{33... | collective-permute-start | bytes 196616 | tf_op jit(solution)/shard_map/ppermute | solution.py:17
  247.0 11.9 %collective-permute-start.26 = (f32[2,2,1024]{2,0,1:T(2,128)S(1)}, f32[2,2,1024]{2,0,1:T(2,128)}, u32[]{:S(2)}, u32[]{:S(2)}) collective-permute-start(f32[2,2,1024]{2,0,1:T(2,128)S(1)} %pad_maximum_fusion.30), channel_id=1, source_target_pairs={{0,1},{1,2},{2,3},{3,4},{4,5},{5,6},{6,7},{7,8},{8,9},{9,10},{10,1... | collective-permute-start | bytes 49160 | tf_op jit(solution)/shard_map/ppermute | solution.py:17
  255.4 5.8 %collective-permute-start.27 = (f32[2,2,1,4096]{3,1,2,0:T(2,128)}, f32[2,2,1,4096]{3,1,2,0:T(2,128)S(1)}, u32[]{:S(2)}, u32[]{:S(2)}) collective-permute-start(f32[2,2,1,4096]{3,1,2,0:T(2,128)} %pad_maximum_fusion.14), channel_id=1, source_target_pairs={{0,16},{16,32},{32,48},{48,64},{64,80},{80,96},{96,112},{1,17},{17... | collective-permute-start | bytes 196616 | tf_op jit(solution)/shard_map/ppermute | solution.py:17
  268.2 12.4 %collective-permute-start.29 = (f32[2,2,1024]{2,0,1:T(2,128)S(1)}, f32[2,2,1024]{2,0,1:T(2,128)}, u32[]{:S(2)}, u32[]{:S(2)}) collective-permute-start(f32[2,2,1024]{2,0,1:T(2,128)S(1)} %pad_maximum_fusion.31), channel_id=1, source_target_pairs={{1,0},{2,1},{3,2},{4,3},{5,4},{6,5},{7,6},{8,7},{9,8},{10,9},{11,1... | collective-permute-start | bytes 49160 | tf_op jit(solution)/shard_map/ppermute | solution.py:17
  287.7 10.2 %collective-permute-start.30 = (f32[2,2,1024]{2,0,1:T(2,128)S(1)}, f32[2,2,1024]{2,0,1:T(2,128)S(1)}, u32[]{:S(2)}, u32[]{:S(2)}) collective-permute-start(f32[2,2,1024]{2,0,1:T(2,128)S(1)} %pad_maximum_fusion.32), channel_id=1, source_target_pairs={{0,1},{1,2},{2,3},{3,4},{4,5},{5,6},{6,7},{7,8},{8,9},{9,10},{10,1... | collective-permute-start | bytes 49160 | tf_op jit(solution)/shard_map/ppermute | solution.py:17
  293.8 5.6 %collective-permute-start.31 = (f32[2,2,1,4096]{3,1,2,0:T(2,128)S(1)}, f32[2,2,1,4096]{3,1,2,0:T(2,128)S(1)}, u32[]{:S(2)}, u32[]{:S(2)}) collective-permute-start(f32[2,2,1,4096]{3,1,2,0:T(2,128)S(1)} %pad_maximum_fusion.16), channel_id=1, source_target_pairs={{0,16},{16,32},{32,48},{48,64},{64,80},{80,96},{96,112},{1,17},{17... | collective-permute-start | bytes 196616 | tf_op jit(solution)/shard_map/ppermute | solution.py:17
  324.1 23.7 %all-to-all-start.1 = ((f32[16,4,2,512]{3,1,2,0:T(4,128)}), f32[16,4,2,512]{3,1,2,0:T(4,128)S(1)}, u32[]{:S(2)}, u32[]{:S(2)}) async-start(f32[16,4,2,512]{3,1,2,0:T(4,128)} %copy.57), calls=%async_computation.1 | async-start | bytes 524288 | tf_op jit(solution)/shard_map/all_to_all | solution.py:182
  (90 other events, 665.4 us)
